TPU v7x, 128 devices: a whole 4x4x4 slice. The times are simulated.
128 devices in a mesh: leaf: 64 (over y_hi, x, z, core), rhs: 2 (over y_lo).
Axes of the slice: x: 4, y: 4 (y_hi: 2, y_lo: 2; y = y_hi * 2 + y_lo), z: 4, core: 2. Of those that a mesh axis runs over, the one named last changes fastest.
Arguments:
- rhs: bfloat16 [524288, 512], P('leaf', 'rhs'), may hold values from -6 to 6
- source_basis: bfloat16 [4096, 128, 128], P('leaf', None, 'rhs'), may hold values from -0.5 to 0.5
- target_basis: bfloat16 [4096, 128, 128], P('leaf', None, 'rhs'), may hold values from -0.5 to 0.5
- near_blocks: bfloat16 [4096, 2, 128, 128], P('leaf', None, None, 'rhs'), may hold values from -0.375 to 0.375
- near_offsets: int32 [4096, 2], P('leaf'), may hold values from -2 to 2
- source_values: bfloat16 [3, 2048, 2, 2, 128, 128], P(None, 'leaf', None, None, 'rhs'), may hold values from -0.375 to 0.375
- source_scales: float32 [3, 2048, 2, 2, 128], P(None, 'leaf'), may hold values from 0.2 to 2
- target_values: bfloat16 [3, 2048, 2, 2, 128, 128], P(None, 'leaf', None, None, 'rhs'), may hold values from -0.375 to 0.375
- target_scales: float32 [3, 2048, 2, 2, 128], P(None, 'leaf'), may hold values from 0.2 to 2
Outputs:
- product: bfloat16 [524288, 512], P('leaf', 'rhs')
All inputs are finite; a program needn't handle non-finite values.
Results may differ from a plain program's by a relative error of at most 0.01.
Values may be sent and summed in bfloat16 or wider, within the bound.
A program may use at most 192 MiB of HBM per device.

v0:
```python
import jax
import jax.numpy as jnp
from jax import lax
from jax.sharding import PartitionSpec as P

REACH = 2
SRC_LEVELS = 3
TGT_LEVELS = 3


def padded_2(cells, sides, width):
    for axis, dim in sides:
        count = lax.axis_size(axis)
        ends = count - 1
        head = lax.slice_in_dim(cells, 0, width, axis=dim)
        tail = lax.slice_in_dim(cells, cells.shape[dim] - width, cells.shape[dim], axis=dim)
        cells = jnp.concatenate(
            [
                lax.ppermute(tail, axis, [(i, (i + 1) % count) for i in range(ends)]),
                cells,
                lax.ppermute(head, axis, [((i + 1) % count, i) for i in range(ends)]),
            ],
            axis=dim,
        )
    return cells


def dequantize(values, scales):
    return (values.astype(jnp.float32) * scales[..., None, :]).astype(jnp.bfloat16)


def butterfly_level(coefficients, blocks, bit_index):
    box_total, columns, rank = coefficients.shape
    outputs = blocks.shape[-2]
    low_span = 2**bit_index
    high_span = box_total // (2 * low_span)
    inputs = coefficients.reshape(high_span, 2, low_span, columns, rank)
    matrices = blocks.reshape(high_span, low_span, 2, 2, outputs, rank)
    mixed = jnp.einsum("hclnr,hlocsr->holns", inputs, matrices, preferred_element_type=jnp.float32)
    return mixed.reshape(box_total, columns, outputs).astype(jnp.bfloat16)


def apply_level(coefficients, scales, bit_index, gathered):
    return butterfly_level(coefficients, dequantize(gathered, scales), bit_index)


def on_device(
    rhs,
    source_basis,
    target_basis,
    near_blocks,
    near_offsets,
    source_values,
    source_scales,
    target_values,
    target_scales,
):
    box_count = source_basis.shape[0]
    box_rows = source_basis.shape[1]
    columns = rhs.shape[1]
    rhs_boxes = rhs.reshape(box_count, box_rows, columns)
    basis_in, basis_out, near_full = (
        lax.all_gather(source_basis, "rhs", axis=2, tiled=True),
        lax.all_gather(target_basis, "rhs", axis=2, tiled=True),
        lax.all_gather(near_blocks, "rhs", axis=3, tiled=True),
    )
    source_tables, target_tables = (
        lax.all_gather(source_values, "rhs", axis=4, tiled=True),
        lax.all_gather(target_values, "rhs", axis=4, tiled=True),
    )
    coefficients = jnp.einsum(
        "bmc,bmr->bcr", rhs_boxes, basis_in, preferred_element_type=jnp.float32
    ).astype(jnp.bfloat16)
    for level_index in range(SRC_LEVELS):
        coefficients = apply_level(
            coefficients, source_scales[level_index], level_index, source_tables[level_index]
        )
    padded = padded_2(rhs_boxes, (("leaf", 0),), REACH)
    source_index = jnp.arange(box_count, dtype=jnp.int32)[:, None] + REACH + near_offsets
    selected = jnp.take(padded, source_index, axis=0)
    near_field = jnp.einsum(
        "bkmn,bknc->bmc", near_full, selected, preferred_element_type=jnp.float32
    )
    row_coefficients = lax.all_to_all(coefficients, "leaf", split_axis=0, concat_axis=0, tiled=True)
    for level_index in range(TGT_LEVELS):
        row_coefficients = apply_level(
            row_coefficients, target_scales[level_index], level_index, target_tables[level_index]
        )
    far_field = jnp.einsum(
        "bmr,bcr->bmc", basis_out, row_coefficients, preferred_element_type=jnp.float32
    )
    return (far_field + near_field).astype(jnp.bfloat16).reshape(box_count * box_rows, columns)


def solution(mesh):
    placed = (
        P("leaf", "rhs"),
        P("leaf", None, "rhs"),
        P("leaf", None, "rhs"),
        P("leaf", None, None, "rhs"),
        P("leaf", None),
        P(None, "leaf", None, None, "rhs", None),
        P(None, "leaf", None, None, None),
        P(None, "leaf", None, None, "rhs", None),
        P(None, "leaf", None, None, None),
    )
    return jax.shard_map(
        on_device, mesh=mesh, in_specs=placed, out_specs=P("leaf", "rhs"), check_vma=False
    )
```

profile of v0, /device:TPU:1, one launch (start us, length us, event | category | flops | bytes accessed | tf_op | source)
XLA Modules:
  0.0 526.6 jit_solution(11540010097013420315)
XLA Ops:
  9.0 38.7 %all-gather.10.cloned.1.call-done = bf16[64,128,128]{1,2,0:T(8,128)(2,1)} async-done(((bf16[64,128,64]{1,2,0:T(8,128)(2,1)}), bf16[64,128,128]{1,2,0:T(8,128)(2,1)}) %all-gather.10.cloned.1.call-update) | async-done | bytes 2097168 | tf_op jit(solution)/shard_map/all_gather | solution.py:63
  47.7 6.2 %convolution_convert_fusion = bf16[64,256,128]{2,1,0:T(8,128)(2,1)} fusion(bf16[64,128,256]{2,1,0:T(8,128)(2,1)} %bitcast.118, bf16[64,128,128]{1,2,0:T(8,128)(2,1)} %all-gather.10.cloned.1.call-done), kind=kOutput, calls=%fused_computation.48 | convolution fusion | flops 538968064 | bytes 10485760 | tf_op jit(solution)/shard_map/bmc,bmr->bcr/dot_general | solution.py:71
  53.9 151.5 %all-gather.8.cloned.1.call-done = bf16[3,32,2,2,128,128]{5,4,3,2,1,0:T(8,128)(2,1)} async-done(((bf16[3,32,2,2,64,128]{5,4,3,2,1,0:T(8,128)(2,1)}), bf16[3,32,2,2,128,128]{5,4,3,2,1,0:T(8,128)(2,1)}) %all-gather.8.cloned.1.call-update) | async-done | bytes 12582928 | tf_op jit(solution)/shard_map/all_gather | solution.py:68
  205.4 5.4 %fusion.61 = (bf16[1,32,2,2,128,128]{5,4,3,2,1,0:T(8,128)(2,1)}, bf16[1,32,2,2,128,128]{5,4,3,2,1,0:T(8,128)(2,1)S(1)}) fusion(bf16[3,32,2,2,128,128]{5,4,3,2,1,0:T(8,128)(2,1)} %all-gather.8.cloned.1.call-done), kind=kLoop, calls=%fused_computation.57 | loop fusion | bytes 16777216 | tf_op jit(solution)/shard_map/slice | solution.py:76
  211.5 3.5 bitcast_convert_fusion.5
  215.0 3.6 fusion.10
  218.6 6.9 %copy.17 = bf16[16,2,2,256,128]{4,3,2,1,0:T(8,128)(2,1)} copy(bf16[16,2,2,256,128]{3,4,1,2,0:T(8,128)(2,1)} %fusion.10) | data formatting | bytes 8388608 | tf_op jit(solution)/shard_map/convert_element_type | solution.py:40
  225.6 7.4 %fusion.11 = bf16[8,2,4,256,128]{3,4,1,2,0:T(8,128)(2,1)} fusion(bf16[8,2,4,256,128,1]{4,3,2,1,0,5:T(8,128)(2,1)} %bitcast.123, bf16[8,4,2,2,128,128]{5,4,3,2,1,0:T(8,128)(2,1)} %bitcast.126, f32[8,4,2,2,128]{4,3,2,1,0:T(2,128)S(1)} %bitcast.133), kind=kOutput, calls=%fused_computation.26 | convolution fusion | flops 1082130432 | bytes 12648448 | tf_op jit(solution)/shard_map/hclnr,hlocsr->holns/dot_general | solution.py:39
  233.0 6.5 %copy.19 = bf16[8,2,4,256,128]{4,3,2,1,0:T(8,128)(2,1)} copy(bf16[8,2,4,256,128]{3,4,1,2,0:T(8,128)(2,1)} %fusion.11) | data formatting | bytes 8388608 | tf_op jit(solution)/shard_map/convert_element_type | solution.py:40
  239.5 10.7 %all-to-all-start = ((bf16[64,256,128]{2,1,0:T(8,128)(2,1)}), bf16[64,256,128]{2,1,0:T(8,128)(2,1)}, u32[]{:S(2)}, u32[]{:S(2)}) async-start(bf16[64,256,128]{2,1,0:T(8,128)(2,1)} %bitcast.121), calls=%async_computation | async-start | bytes 8388608 | tf_op jit(solution)/shard_map/all_to_all | solution.py:84
  252.4 3.5 collective-permute-start
  258.5 13.0 %collective-permute-done = bf16[2,128,256]{2,1,0:T(8,128)(2,1)S(1)} collective-permute-done((bf16[2,128,256]{2,1,0:T(8,128)(2,1)S(1)}, bf16[2,128,256]{2,1,0:T(8,128)(2,1)S(1)}, u32[]{:S(2)}, u32[]{:S(2)}) %collective-permute-start) | collective-permute-done | bytes 131104 | tf_op jit(solution)/shard_map/ppermute | solution.py:19
  273.7 4.0 pad_maximum_fusion
  277.7 8.8 %gather_fusion = bf16[128,128,256]{2,1,0:T(8,128)(2,1)} fusion(bf16[68,128,256]{2,1,0:T(8,128)(2,1)} %pad_maximum_fusion, s32[1024]{0:T(1024)S(1)} %pad_clamp_fusion), kind=kCustom, calls=%fused_computation | custom fusion | bytes 16777728 | tf_op jit(solution)/shard_map/jit(_take)/gather | solution.py:80
  286.5 121.5 %all-gather.6.cloned.1.call-done = bf16[3,32,2,2,128,128]{5,4,3,2,1,0:T(8,128)(2,1)} async-done(((bf16[3,32,2,2,64,128]{5,4,3,2,1,0:T(8,128)(2,1)}), bf16[3,32,2,2,128,128]{5,4,3,2,1,0:T(8,128)(2,1)}) %all-gather.6.cloned.1.call-update) | async-done | bytes 12582928 | tf_op jit(solution)/shard_map/all_gather | solution.py:69
  408.0 6.2 %fusion.60 = (bf16[1,32,2,2,128,128]{5,4,3,2,1,0:T(8,128)(2,1)}, bf16[1,32,2,2,128,128]{5,4,3,2,1,0:T(8,128)(2,1)}) fusion(bf16[3,32,2,2,128,128]{5,4,3,2,1,0:T(8,128)(2,1)} %all-gather.6.cloned.1.call-done), kind=kLoop, calls=%fused_computation.56 | loop fusion | bytes 16777216 | tf_op jit(solution)/shard_map/slice | solution.py:87
  414.2 4.9 bitcast_convert_fusion.2
  422.4 6.6 %copy.21 = bf16[16,2,2,256,128]{4,3,2,1,0:T(8,128)(2,1)} copy(bf16[16,2,2,256,128]{3,4,1,2,0:T(8,128)(2,1)} %fusion.12) | data formatting | bytes 8388608 | tf_op jit(solution)/shard_map/convert_element_type | solution.py:40
  429.0 6.7 %fusion.13 = bf16[8,2,4,256,128]{3,4,1,2,0:T(8,128)(2,1)} fusion(bf16[8,2,4,256,128,1]{4,3,2,1,0,5:T(8,128)(2,1)} %bitcast.124, bf16[8,4,2,2,128,128]{5,4,3,2,1,0:T(8,128)(2,1)} %bitcast.125, f32[8,4,2,2,128]{4,3,2,1,0:T(2,128)S(1)} %bitcast.131), kind=kOutput, calls=%fused_computation.28 | convolution fusion | flops 1082130432 | bytes 12648448 | tf_op jit(solution)/shard_map/hclnr,hlocsr->holns/dot_general | solution.py:39
  435.7 6.4 %copy.23 = bf16[8,2,4,256,128]{4,3,2,1,0:T(8,128)(2,1)} copy(bf16[8,2,4,256,128]{3,4,1,2,0:T(8,128)(2,1)} %fusion.13) | data formatting | bytes 8388608 | tf_op jit(solution)/shard_map/convert_element_type | solution.py:40
  442.1 6.1 %all-gather.12.cloned.1.call-done = bf16[64,128,128]{1,2,0:T(8,128)(2,1)} async-done(((bf16[64,128,64]{1,2,0:T(8,128)(2,1)}), bf16[64,128,128]{1,2,0:T(8,128)(2,1)}) %all-gather.12.cloned.1.call-update) | async-done | bytes 2097168 | tf_op jit(solution)/shard_map/all_gather | solution.py:64
  448.3 7.4 %fusion.65 = f32[64,256,128]{1,2,0:T(8,128)} fusion(bf16[64,256,128]{2,1,0:T(8,128)(2,1)} %bitcast.120, bf16[64,128,128]{1,2,0:T(8,128)(2,1)} %all-gather.12.cloned.1.call-done), kind=kOutput, calls=%fused_computation.61 | convolution fusion | flops 536870912 | bytes 14680064 | tf_op jit(solution)/shard_map/bmr,bcr->bmc/dot_general | solution.py:89
  455.7 54.3 %all-gather.14.cloned.1.call-done = bf16[64,2,128,128]{2,3,1,0:T(8,128)(2,1)} async-done(((bf16[64,2,128,64]{2,3,1,0:T(8,128)(2,1)}), bf16[64,2,128,128]{2,3,1,0:T(8,128)(2,1)}) %all-gather.14.cloned.1.call-update) | async-done | bytes 4194320 | tf_op jit(solution)/shard_map/all_gather | solution.py:65
  510.0 10.1 %fusion.6 = bf16[64,256,128]{1,2,0:T(8,128)(2,1)} fusion(f32[64,256,128]{1,2,0:T(8,128)} %fusion.65, bf16[64,2,128,128]{2,3,1,0:T(8,128)(2,1)} %all-gather.14.cloned.1.call-done, bf16[64,2,128,256]{3,2,1,0:T(8,128)(2,1)} %bitcast.117, pred[64,2]{1,0:T(8,128)(4,1)S(1)} %copy.24), kind=kOutput, calls=%fused_computation.14 | convolution fusion | flops 1082130432 | bytes 25165952 | tf_op jit(solution)/shard_map/bkmn,bknc->bmc/dot_general | solution.py:81
  (33 shorter events, 13.2 us)
Async XLA Ops:
  6.5 41.1 %all-gather.10.cloned.1.call-start = ((), (), s32[]{:S(2)}) async-start(), calls=%async_computation.3 | async-start | bytes 3145728 | tf_op jit(solution)/shard_map/all_gather | solution.py:63
  7.3 198.1 %all-gather.8.cloned.1.call-start = ((), (), s32[]{:S(2)}) async-start(), calls=%async_computation.2 | async-start | bytes 18874368 | tf_op jit(solution)/shard_map/all_gather | solution.py:68
  8.0 0.9 copy-start.2
  8.0 400.0 %all-gather.6.cloned.1.call-start = ((), (), s32[]{:S(2)}) async-start(), calls=%async_computation.1 | async-start | bytes 18874368 | tf_op jit(solution)/shard_map/all_gather | solution.py:69
  205.4 6.2 %copy-start = (bf16[64,256,128]{2,1,0:T(8,128)(2,1)S(1)}, bf16[64,256,128]{2,1,0:T(8,128)(2,1)}, u32[]{:S(2)}) copy-start(bf16[64,256,128]{2,1,0:T(8,128)(2,1)} %convolution_convert_fusion) | copy-start | bytes 12582916
  239.5 18.6 %copy-start.3 = (f32[3,32,2,2,128]{4,3,2,1,0:T(2,128)S(1)}, f32[3,32,2,2,128]{4,3,2,1,0:T(2,128)}, u32[]{:S(2)}) copy-start(f32[3,32,2,2,128]{4,3,2,1,0:T(2,128)} %param.17) | copy-start | bytes 589828
  239.5 18.6 %copy-start.4 = (s32[64,2]{0,1:T(2,128)S(1)}, s32[64,2]{0,1:T(2,128)}, u32[]{:S(2)}) copy-start(s32[64,2]{0,1:T(2,128)} %param.13) | copy-start | bytes 1540
  239.5 174.7 %all-to-all-start = ((bf16[64,256,128]{2,1,0:T(8,128)(2,1)}), bf16[64,256,128]{2,1,0:T(8,128)(2,1)}, u32[]{:S(2)}, u32[]{:S(2)}) async-start(bf16[64,256,128]{2,1,0:T(8,128)(2,1)} %bitcast.121), calls=%async_computation | async-start | bytes 8388608 | tf_op jit(solution)/shard_map/all_to_all | solution.py:84
  250.3 198.0 %all-gather.12.cloned.1.call-start = ((), (), s32[]{:S(2)}) async-start(), calls=%async_computation.4 | async-start | bytes 3145728 | tf_op jit(solution)/shard_map/all_gather | solution.py:64
  250.8 259.2 %all-gather.14.cloned.1.call-start = ((), (), s32[]{:S(2)}) async-start(), calls=%async_computation.5 | async-start | bytes 6291456 | tf_op jit(solution)/shard_map/all_gather | solution.py:65
  252.4 19.1 %collective-permute-start = (bf16[2,128,256]{2,1,0:T(8,128)(2,1)S(1)}, bf16[2,128,256]{2,1,0:T(8,128)(2,1)S(1)}, u32[]{:S(2)}, u32[]{:S(2)}) collective-permute-start(bf16[2,128,256]{2,1,0:T(8,128)(2,1)S(1)} %bitcast.130), channel_id=1, source_target_pairs={{0,2},{2,4},{4,6},{6,8},{8,10},{10,12},{12,14},{14,16},{16,18},{18... | collective-permute-start | bytes 393224 | tf_op jit(solution)/shard_map/ppermute | solution.py:19
  256.0 17.8 %collective-permute-start.1 = (bf16[2,128,256]{2,1,0:T(8,128)(2,1)S(1)}, bf16[2,128,256]{2,1,0:T(8,128)(2,1)S(1)}, u32[]{:S(2)}, u32[]{:S(2)}) collective-permute-start(bf16[2,128,256]{2,1,0:T(8,128)(2,1)S(1)} %bitcast.129), channel_id=1, source_target_pairs={{2,0},{4,2},{6,4},{8,6},{10,8},{12,10},{14,12},{16,14},{18,16},{20... | collective-permute-start | bytes 393224 | tf_op jit(solution)/shard_map/ppermute | solution.py:21
  414.2 4.9 copy-start.1
Sparse Core Ops, SparseCore 0:
  9.0 38.6 all-gather.9
  49.3 155.9 all-gather.7
  207.0 200.9 all-gather.5
  409.5 38.7 all-gather.11
  449.8 60.2 all-gather.13
where the time goes:
time: 528 us; the launch traced here: 527 us
  waiting for transfers between devices  391 us (74%)
  matrix products  53.1 us (10%)
  local copies, waits for them, and re-layouts  49.3 us (9%)
  starting transfers between devices  16.5 us (3%)
  between operations  13.3 us (3%)
    all_gather x1, waiting for transfers between devices, on_device(): lax.all_gather(source_values, 'rhs', axis=4, tiled=True)  152 us
    all_gather x1, waiting for transfers between devices, on_device(): lax.all_gather(target_values, 'rhs', axis=4, tiled=True)  121 us
    all_gather x1, waiting for transfers between devices, on_device(): lax.all_gather(near_blocks, 'rhs', axis=3, tiled=True)  54.3 us
    all_gather x1, waiting for transfers between devices, on_device(): lax.all_gather(source_basis, 'rhs', axis=2, tiled=True)  38.7 us
    dot_general x6, matrix products, butterfly_level(): jnp.einsum('hclnr,hlocsr->holns', inputs, matrices, preferred_element_typ...  29.3 us
    convert_element_type x4, local copies, waits for them, and re-layouts, butterfly_level(): return mixed.reshape(box_total, columns, outputs).astype(jnp.bfloat16)  26.5 us
    ppermute x1, waiting for transfers between devices, padded_2(): lax.ppermute(tail, axis, [(i, (i + 1) % count) for i in range(ends)])  13 us
    all_to_all x1, starting transfers between devices, on_device(): lax.all_to_all(coefficients, 'leaf', split_axis=0, concat_axis=0, tiled=T...  10.7 us
  transfers between devices with their start and end apart: 8, of which 7 were waited for; matrix products, arithmetic and copies ran while one was open for 18% of the time, Pallas kernels for 0%

commit v1 on v0

--- a/solution.py
+++ b/solution.py
@@ -6,6 +6,11 @@
 REACH = 2
 SRC_LEVELS = 3
 TGT_LEVELS = 3
+
+
+def swapped_in(value, axis, along):
+    outgoing = jnp.stack([value] * lax.axis_size(axis))
+    return jnp.concatenate(lax.all_to_all(outgoing, axis, 0, 0), axis=along)
 
 
 def padded_2(cells, sides, width):
@@ -65,7 +70,7 @@
         lax.all_gather(near_blocks, "rhs", axis=3, tiled=True),
     )
     source_tables, target_tables = (
-        lax.all_gather(source_values, "rhs", axis=4, tiled=True),
+        swapped_in(source_values, "rhs", 4),
         lax.all_gather(target_values, "rhs", axis=4, tiled=True),
     )
     coefficients = jnp.einsum(

time: 528 us -> 483 us (0.915)
  waiting for transfers between devices: 391 us -> 318 us
  other arithmetic: 3.97 us -> 15.1 us
  starting transfers between devices: 16.5 us -> 26 us
  local copies, waits for them, and re-layouts: 49.3 us -> 56.7 us
    all_to_all x0 -> x1, waiting for transfers between devices: none -> 210 us  [swapped_in(): return jnp.concatenate(lax.all_to_all(outgoing, axis, 0, 0), axis=along)]
    all_gather x1 -> x0, waiting for transfers between devices: 152 us -> none  [on_device(): lax.all_gather(source_values, 'rhs', axis=4, tiled=True)]
    all_gather x1, waiting for transfers between devices: 121 us -> 0.01 us  [on_device(): lax.all_gather(target_values, 'rhs', axis=4, tiled=True)]
    ppermute x1, waiting for transfers between devices: 13 us -> 32.9 us  [padded_2(): lax.ppermute(tail, axis, [(i, (i + 1) % count) for i in range(ends)])]
    all_gather x1, waiting for transfers between devices: 54.3 us -> 37.7 us  [on_device(): lax.all_gather(near_blocks, 'rhs', axis=3, tiled=True)]
    another operation x0 -> x1, other arithmetic: none -> 11 us  [swapped_in(): outgoing = jnp.stack([value] * lax.axis_size(axis))]
    all_to_all x0 -> x1, starting transfers between devices: none -> 8.95 us  [swapped_in(): return jnp.concatenate(lax.all_to_all(outgoing, axis, 0, 0), axis=along)]
    all_to_all x0 -> x1, local copies, waits for them, and re-layouts: none -> 6.54 us  [swapped_in(): return jnp.concatenate(lax.all_to_all(outgoing, axis, 0, 0), axis=along)]
  transfers between devices with their start and end apart: 8 -> 8, of which waited for: 7 -> 4; matrix products, arithmetic and copies ran while one was open for 18% -> 24% of each run, Pallas kernels for 0% -> 0%
where the time goes in v1:
time: 483 us; the launch traced here: 482 us
  waiting for transfers between devices  318 us (66%)
  local copies, waits for them, and re-layouts  56.7 us (12%)
  matrix products  52.6 us (11%)
  starting transfers between devices  26 us (5%)
  other arithmetic  15.1 us (3%)
  between operations  13.3 us (3%)
    all_to_all x1, waiting for transfers between devices, swapped_in(): return jnp.concatenate(lax.all_to_all(outgoing, axis, 0, 0), axis=along)  210 us
    all_gather x1, waiting for transfers between devices, on_device(): lax.all_gather(near_blocks, 'rhs', axis=3, tiled=True)  37.7 us
    all_gather x1, waiting for transfers between devices, on_device(): lax.all_gather(source_basis, 'rhs', axis=2, tiled=True)  35.1 us
    ppermute x1, waiting for transfers between devices, padded_2(): lax.ppermute(tail, axis, [(i, (i + 1) % count) for i in range(ends)])  32.9 us
    dot_general x6, matrix products, butterfly_level(): jnp.einsum('hclnr,hlocsr->holns', inputs, matrices, preferred_element_typ...  28.4 us
    convert_element_type x4, local copies, waits for them, and re-layouts, butterfly_level(): return mixed.reshape(box_total, columns, outputs).astype(jnp.bfloat16)  25.9 us
    all_to_all x1, starting transfers between devices, on_device(): lax.all_to_all(coefficients, 'leaf', split_axis=0, concat_axis=0, tiled=T...  11.2 us
    another operation x1, other arithmetic, swapped_in(): outgoing = jnp.stack([value] * lax.axis_size(axis))  11 us
  transfers between devices with their start and end apart: 8, of which 4 were waited for; matrix products, arithmetic and copies ran while one was open for 24% of the time, Pallas kernels for 0%

profile of v1, /device:TPU:1, one launch (start us, length us, event | category | flops | bytes accessed | tf_op | source)
XLA Modules:
  0.0 481.9 jit_solution(8543133722382979047)
XLA Ops:
  8.0 11.0 %pad_maximum_fusion = bf16[2,3,32,2,2,64,128]{6,5,4,3,2,1,0:T(8,128)(2,1)} fusion(bf16[1,3,32,2,2,64,128]{6,5,4,3,2,1,0:T(8,128)(2,1)} %bitcast.123), kind=kLoop, calls=%fused_computation.1 | loop fusion | flops 6291456 | bytes 18874368 | tf_op jit(solution)/shard_map/stack | solution.py:12
  19.0 8.9 %all-to-all-start = ((bf16[2,3,32,2,2,64,128]{6,5,4,3,2,1,0:T(8,128)(2,1)}), bf16[2,3,32,2,2,64,128]{6,5,4,3,2,1,0:T(8,128)(2,1)}, u32[]{:S(2)}, u32[]{:S(2)}) async-start(bf16[2,3,32,2,2,64,128]{6,5,4,3,2,1,0:T(8,128)(2,1)} %pad_maximum_fusion), calls=%async_computation | async-start | bytes 25165824 | tf_op jit(solution)/shard_map/all_to_all | solution.py:13
  28.0 35.1 %all-gather.7.cloned.1.call-done = bf16[64,128,128]{1,2,0:T(8,128)(2,1)} async-done(((bf16[64,128,64]{1,2,0:T(8,128)(2,1)}), bf16[64,128,128]{1,2,0:T(8,128)(2,1)}) %all-gather.7.cloned.1.call-update) | async-done | bytes 2097168 | tf_op jit(solution)/shard_map/all_gather | solution.py:68
  63.1 6.2 %convolution_convert_fusion = bf16[64,256,128]{2,1,0:T(8,128)(2,1)} fusion(bf16[64,128,256]{2,1,0:T(8,128)(2,1)} %bitcast.117, bf16[64,128,128]{1,2,0:T(8,128)(2,1)} %all-gather.7.cloned.1.call-done), kind=kOutput, calls=%fused_computation.49 | convolution fusion | flops 538968064 | bytes 10485760 | tf_op jit(solution)/shard_map/bmc,bmr->bcr/dot_general | solution.py:76
  69.3 209.9 %all-to-all-done = bf16[2,3,32,2,2,64,128]{6,5,4,3,2,1,0:T(8,128)(2,1)} async-done(((bf16[2,3,32,2,2,64,128]{6,5,4,3,2,1,0:T(8,128)(2,1)}), bf16[2,3,32,2,2,64,128]{6,5,4,3,2,1,0:T(8,128)(2,1)}, u32[]{:S(2)}, u32[]{:S(2)}) %all-to-all-start) | async-done | bytes 12582944 | tf_op jit(solution)/shard_map/all_to_all | solution.py:13
  279.2 6.5 %copy.77 = bf16[2,3,32,2,2,64,128]{6,5,0,4,3,2,1:T(8,128)(2,1)S(1)} copy(bf16[2,3,32,2,2,64,128]{6,5,4,3,2,1,0:T(8,128)(2,1)} %all-to-all-done) | data formatting | bytes 25165824 | tf_op jit(solution)/shard_map/all_to_all | solution.py:13
  285.7 7.9 %fusion.61 = (bf16[1,32,2,2,2,64,128]{6,5,4,3,2,1,0:T(8,128)(2,1)}, bf16[1,32,2,2,2,64,128]{6,5,4,3,2,1,0:T(8,128)(2,1)S(1)}, bf16[1,32,2,2,2,64,128]{6,5,4,3,2,1,0:T(8,128)(2,1)}) fusion(bf16[3,32,2,2,2,64,128]{6,5,4,3,2,1,0:T(8,128)(2,1)S(1)} %bitcast.115), kind=kLoop, calls=%fused_computation.58 | loop fusion | bytes 25165824 | tf_op jit(solution)/shard_map/slice | solution.py:81
  294.9 5.5 %fusion.10 = bf16[16,2,2,256,128]{3,4,1,2,0:T(8,128)(2,1)} fusion(bf16[16,2,2,256,128,1]{3,4,2,1,0,5:T(8,128)(2,1)S(1)} %bitcast.124, bf16[16,2,2,2,128,128]{5,4,3,2,1,0:T(8,128)(2,1)} %bitcast.130, f32[16,2,2,2,128]{4,3,2,1,0:T(2,128)S(1)} %bitcast.136), kind=kOutput, calls=%fused_computation.27 | convolution fusion | flops 1082130432 | bytes 12648448 | tf_op jit(solution)/shard_map/hclnr,hlocsr->holns/dot_general | solution.py:44
  300.4 6.4 %copy.29 = bf16[16,2,2,256,128]{4,3,2,1,0:T(8,128)(2,1)} copy(bf16[16,2,2,256,128]{3,4,1,2,0:T(8,128)(2,1)} %fusion.10) | data formatting | bytes 8388608 | tf_op jit(solution)/shard_map/convert_element_type | solution.py:45
  306.7 6.8 %fusion.11 = bf16[8,2,4,256,128]{3,4,1,2,0:T(8,128)(2,1)} fusion(bf16[8,2,4,256,128,1]{4,3,2,1,0,5:T(8,128)(2,1)} %bitcast.125, bf16[8,4,2,2,128,128]{5,4,3,2,1,0:T(8,128)(2,1)} %bitcast.128, f32[8,4,2,2,128]{4,3,2,1,0:T(2,128)S(1)} %bitcast.135), kind=kOutput, calls=%fused_computation.28 | convolution fusion | flops 1082130432 | bytes 12648448 | tf_op jit(solution)/shard_map/hclnr,hlocsr->holns/dot_general | solution.py:44
  313.5 6.4 %copy.31 = bf16[8,2,4,256,128]{4,3,2,1,0:T(8,128)(2,1)} copy(bf16[8,2,4,256,128]{3,4,1,2,0:T(8,128)(2,1)} %fusion.11) | data formatting | bytes 8388608 | tf_op jit(solution)/shard_map/convert_element_type | solution.py:45
  320.0 11.2 %all-to-all-start.1 = ((bf16[64,256,128]{2,1,0:T(8,128)(2,1)}), bf16[64,256,128]{2,1,0:T(8,128)(2,1)}, u32[]{:S(2)}, u32[]{:S(2)}) async-start(bf16[64,256,128]{2,1,0:T(8,128)(2,1)} %bitcast.121), calls=%async_computation.1 | async-start | bytes 8388608 | tf_op jit(solution)/shard_map/all_to_all | solution.py:89
  333.5 3.5 collective-permute-start
  339.6 32.9 %collective-permute-done = bf16[2,128,256]{2,1,0:T(8,128)(2,1)S(1)} collective-permute-done((bf16[2,128,256]{2,1,0:T(8,128)(2,1)S(1)}, bf16[2,128,256]{2,1,0:T(8,128)(2,1)S(1)}, u32[]{:S(2)}, u32[]{:S(2)}) %collective-permute-start) | collective-permute-done | bytes 131104 | tf_op jit(solution)/shard_map/ppermute | solution.py:24
  372.5 4.1 pad_maximum_fusion.1
  376.6 8.8 %gather_fusion = bf16[128,128,256]{2,1,0:T(8,128)(2,1)} fusion(bf16[68,128,256]{2,1,0:T(8,128)(2,1)} %pad_maximum_fusion.1, s32[1024]{0:T(1024)S(1)} %pad_clamp_fusion), kind=kCustom, calls=%fused_computation | custom fusion | bytes 16777728 | tf_op jit(solution)/shard_map/jit(_take)/gather | solution.py:85
  385.4 6.2 %fusion.60 = (bf16[1,32,2,2,128,128]{5,4,3,2,1,0:T(8,128)(2,1)}, bf16[1,32,2,2,128,128]{5,4,3,2,1,0:T(8,128)(2,1)}) fusion(bf16[3,32,2,2,128,128]{5,4,3,2,1,0:T(8,128)(2,1)} %all-gather.5.cloned.1.call-done), kind=kLoop, calls=%fused_computation.57 | loop fusion | bytes 16777216 | tf_op jit(solution)/shard_map/slice | solution.py:92
  391.6 4.9 %bitcast_convert_fusion.2 = bf16[32,2,128,256]{3,2,1,0:T(8,128)(2,1)S(1)} fusion(bf16[32,2,256,128,1]{3,2,1,4,0:T(8,128)(2,1)} %bitcast.35, bf16[3,32,2,2,128,128]{5,4,3,2,1,0:T(8,128)(2,1)} %all-gather.5.cloned.1.call-done, f32[32,2,2,128]{3,2,1,0:T(2,128)S(1)} %get-tuple-element.15), kind=kOutput, calls=%fused_computation.19 | convolution fusion | flops 1082130432 | bytes 12648448 | tf_op jit(solution)/shard_map/hclnr,hlocsr->holns/dot_general | solution.py:44
  399.7 6.5 %copy.33 = bf16[16,2,2,256,128]{4,3,2,1,0:T(8,128)(2,1)} copy(bf16[16,2,2,256,128]{3,4,1,2,0:T(8,128)(2,1)} %fusion.12) | data formatting | bytes 8388608 | tf_op jit(solution)/shard_map/convert_element_type | solution.py:45
  406.2 6.7 %fusion.13 = bf16[8,2,4,256,128]{3,4,1,2,0:T(8,128)(2,1)} fusion(bf16[8,2,4,256,128,1]{4,3,2,1,0,5:T(8,128)(2,1)} %bitcast.126, bf16[8,4,2,2,128,128]{5,4,3,2,1,0:T(8,128)(2,1)} %bitcast.127, f32[8,4,2,2,128]{4,3,2,1,0:T(2,128)S(1)} %bitcast.133), kind=kOutput, calls=%fused_computation.30 | convolution fusion | flops 1082130432 | bytes 12648448 | tf_op jit(solution)/shard_map/hclnr,hlocsr->holns/dot_general | solution.py:44
  412.9 6.6 %copy.35 = bf16[8,2,4,256,128]{4,3,2,1,0:T(8,128)(2,1)} copy(bf16[8,2,4,256,128]{3,4,1,2,0:T(8,128)(2,1)} %fusion.13) | data formatting | bytes 8388608 | tf_op jit(solution)/shard_map/convert_element_type | solution.py:45
  419.5 8.0 %fusion.65 = f32[64,256,128]{1,2,0:T(8,128)} fusion(bf16[64,256,128]{2,1,0:T(8,128)(2,1)} %bitcast.120, bf16[64,128,128]{1,2,0:T(8,128)(2,1)} %all-gather.9.cloned.1.call-done), kind=kOutput, calls=%fused_computation.62 | convolution fusion | flops 536870912 | bytes 14680064 | tf_op jit(solution)/shard_map/bmr,bcr->bmc/dot_general | solution.py:94
  427.5 37.7 %all-gather.11.cloned.1.call-done = bf16[64,2,128,128]{2,3,1,0:T(8,128)(2,1)} async-done(((bf16[64,2,128,64]{2,3,1,0:T(8,128)(2,1)}), bf16[64,2,128,128]{2,3,1,0:T(8,128)(2,1)}) %all-gather.11.cloned.1.call-update) | async-done | bytes 4194320 | tf_op jit(solution)/shard_map/all_gather | solution.py:70
  465.3 10.1 %fusion.6 = bf16[64,256,128]{1,2,0:T(8,128)(2,1)} fusion(f32[64,256,128]{1,2,0:T(8,128)} %fusion.65, bf16[64,2,128,128]{2,3,1,0:T(8,128)(2,1)} %all-gather.11.cloned.1.call-done, bf16[64,2,128,256]{3,2,1,0:T(8,128)(2,1)} %bitcast.116, pred[64,2]{1,0:T(8,128)(4,1)S(1)} %copy.36), kind=kOutput, calls=%fused_computation.16 | convolution fusion | flops 1082130432 | bytes 25165952 | tf_op jit(solution)/shard_map/bkmn,bknc->bmc/dot_general | solution.py:86
  (34 shorter events, 10.8 us)
Async XLA Ops:
  6.5 56.6 %all-gather.7.cloned.1.call-start = ((), (), s32[]{:S(2)}) async-start(), calls=%async_computation.3 | async-start | bytes 3145728 | tf_op jit(solution)/shard_map/all_gather | solution.py:68
  7.3 378.1 %all-gather.5.cloned.1.call-start = ((), (), s32[]{:S(2)}) async-start(), calls=%async_computation.2 | async-start | bytes 18874368 | tf_op jit(solution)/shard_map/all_gather | solution.py:74
  19.0 9.0 %copy-start.2 = (f32[3,32,2,2,128]{4,3,2,1,0:T(2,128)S(1)}, f32[3,32,2,2,128]{4,3,2,1,0:T(2,128)}, u32[]{:S(2)}) copy-start(f32[3,32,2,2,128]{4,3,2,1,0:T(2,128)} %param.15) | copy-start | bytes 589828
  19.0 260.1 %all-to-all-start = ((bf16[2,3,32,2,2,64,128]{6,5,4,3,2,1,0:T(8,128)(2,1)}), bf16[2,3,32,2,2,64,128]{6,5,4,3,2,1,0:T(8,128)(2,1)}, u32[]{:S(2)}, u32[]{:S(2)}) async-start(bf16[2,3,32,2,2,64,128]{6,5,4,3,2,1,0:T(8,128)(2,1)} %pad_maximum_fusion), calls=%async_computation | async-start | bytes 25165824 | tf_op jit(solution)/shard_map/all_to_all | solution.py:13
  285.7 7.9 %copy-start = (bf16[64,256,128]{2,1,0:T(8,128)(2,1)S(1)}, bf16[64,256,128]{2,1,0:T(8,128)(2,1)}, u32[]{:S(2)}) copy-start(bf16[64,256,128]{2,1,0:T(8,128)(2,1)} %convolution_convert_fusion) | copy-start | bytes 12582916
  320.0 19.2 %copy-start.3 = (f32[3,32,2,2,128]{4,3,2,1,0:T(2,128)S(1)}, f32[3,32,2,2,128]{4,3,2,1,0:T(2,128)}, u32[]{:S(2)}) copy-start(f32[3,32,2,2,128]{4,3,2,1,0:T(2,128)} %param.17) | copy-start | bytes 589828
  320.0 19.3 %copy-start.4 = (s32[64,2]{0,1:T(2,128)S(1)}, s32[64,2]{0,1:T(2,128)}, u32[]{:S(2)}) copy-start(s32[64,2]{0,1:T(2,128)} %param.13) | copy-start | bytes 1540
  320.0 71.6 %all-to-all-start.1 = ((bf16[64,256,128]{2,1,0:T(8,128)(2,1)}), bf16[64,256,128]{2,1,0:T(8,128)(2,1)}, u32[]{:S(2)}, u32[]{:S(2)}) async-start(bf16[64,256,128]{2,1,0:T(8,128)(2,1)} %bitcast.121), calls=%async_computation.1 | async-start | bytes 8388608 | tf_op jit(solution)/shard_map/all_to_all | solution.py:89
  331.2 88.3 %all-gather.9.cloned.1.call-start = ((), (), s32[]{:S(2)}) async-start(), calls=%async_computation.4 | async-start | bytes 3145728 | tf_op jit(solution)/shard_map/all_gather | solution.py:69
  331.9 133.3 %all-gather.11.cloned.1.call-start = ((), (), s32[]{:S(2)}) async-start(), calls=%async_computation.5 | async-start | bytes 6291456 | tf_op jit(solution)/shard_map/all_gather | solution.py:70
  333.5 39.0 %collective-permute-start = (bf16[2,128,256]{2,1,0:T(8,128)(2,1)S(1)}, bf16[2,128,256]{2,1,0:T(8,128)(2,1)S(1)}, u32[]{:S(2)}, u32[]{:S(2)}) collective-permute-start(bf16[2,128,256]{2,1,0:T(8,128)(2,1)S(1)} %bitcast.132), channel_id=1, source_target_pairs={{0,2},{2,4},{4,6},{6,8},{8,10},{10,12},{12,14},{14,16},{16,18},{18... | collective-permute-start | bytes 393224 | tf_op jit(solution)/shard_map/ppermute | solution.py:24
  337.1 35.4 %collective-permute-start.1 = (bf16[2,128,256]{2,1,0:T(8,128)(2,1)S(1)}, bf16[2,128,256]{2,1,0:T(8,128)(2,1)S(1)}, u32[]{:S(2)}, u32[]{:S(2)}) collective-permute-start(bf16[2,128,256]{2,1,0:T(8,128)(2,1)S(1)} %bitcast.131), channel_id=1, source_target_pairs={{2,0},{4,2},{6,4},{8,6},{10,8},{12,10},{14,12},{16,14},{18,16},{20... | collective-permute-start | bytes 393224 | tf_op jit(solution)/shard_map/ppermute | solution.py:26
  391.6 4.9 %copy-start.1 = (bf16[1,32,2,2,128,128]{5,4,3,2,1,0:T(8,128)(2,1)S(1)}, bf16[1,32,2,2,128,128]{5,4,3,2,1,0:T(8,128)(2,1)}, u32[]{:S(2)}) copy-start(bf16[1,32,2,2,128,128]{5,4,3,2,1,0:T(8,128)(2,1)} %get-tuple-element.8) | copy-start | bytes 12582916
Sparse Core Ops, SparseCore 0:
  9.0 54.0 all-gather.6
  64.8 252.7 all-gather.4
  333.7 69.2 all-gather.8
  404.5 60.7 all-gather.10
